TPU v7x, 256 devices: a whole 4x4x8 slice. The times are simulated.
256 devices in a mesh: outer: 8 (over z_hi, y), shard: 32 (over z_lo, x, core).
Axes of the slice: x: 4, y: 4, z: 8 (z_hi: 2, z_lo: 4; z = z_hi * 4 + z_lo), core: 2. Of those that a mesh axis runs over, the one named last changes fastest.
Arguments:
- grad_values: bfloat16 [8, 32, 256, 14848], P('outer', 'shard'), may hold values from -6 to 6
- grad_scales: bfloat16 [8, 32, 256, 116], P('outer', 'shard'), may hold values from 0.029907227 to 0.29882812
- block_owner: int32 [256], replicated, may hold values from 0 to 31, as said below
- projector: bfloat16 [8192, 256], P(('outer', 'shard')), may hold values from -0.375 to 0.375
- weights: bfloat16 [8192, 14848], P(('outer', 'shard')), may hold values from -6 to 6
- first_moment: float32 [256, 14848], P('shard'), may hold values from -6 to 6
- second_moment: float32 [256, 14848], P('shard'), may hold values from 0.5 to 4
Outputs:
- new_weights: bfloat16 [8192, 14848], P(('outer', 'shard'))
- new_first: float32 [256, 14848], P('shard')
- new_second: float32 [256, 14848], P('shard')
Inputs may be any that keep to these rules, and one draw needn't show every extreme that they name: `block_owner`: every index of shard owns exactly 8 rows.
All inputs are finite; a program needn't handle non-finite values.
Results may differ from a plain program's by a relative error of at most 0.0015.
Values may be sent and summed in bfloat16 or wider, within the bound.
A program may use at most 128 MiB of HBM per device.

v0:
```python
import jax
import jax.numpy as jnp
from jax import lax
from jax.sharding import PartitionSpec as P

first_decay = 0.9
second_decay = 0.999
step_count = 100.0
update_scale = 0.25


def per_device(
    grad_values, grad_scales, block_owner, projector, weights, first_moment, second_moment
):
    shards = lax.axis_size("shard")
    rank_rows = block_owner.shape[0]
    owned_rows = rank_rows // shards
    values = grad_values[0, 0]
    scales = grad_scales[0, 0]
    col_blocks = scales.shape[1]
    block_width = values.shape[1] // col_blocks
    row_index = jnp.arange(rank_rows, dtype=jnp.int32)
    sort_keys = block_owner * rank_rows + row_index
    position = jnp.sum((sort_keys[None, :] < sort_keys[:, None]).astype(jnp.int32), axis=1)
    placing = (position[None, :] == row_index[:, None]).astype(jnp.bfloat16)
    sent_values = jnp.dot(placing, values, preferred_element_type=jnp.float32).astype(jnp.bfloat16)
    sent_scales = jnp.dot(placing, scales, preferred_element_type=jnp.float32).astype(jnp.bfloat16)
    got_values, got_scales = (
        lax.all_to_all(
            sent_values.reshape(shards, owned_rows, -1),
            "shard",
            split_axis=0,
            concat_axis=0,
            tiled=True,
        ),
        lax.all_to_all(
            sent_scales.reshape(shards, owned_rows, col_blocks),
            "shard",
            split_axis=0,
            concat_axis=0,
            tiled=True,
        ),
    )
    blocked = got_values.reshape(shards, owned_rows, col_blocks, block_width).astype(jnp.float32)
    pod_sum = jnp.sum(blocked * got_scales.astype(jnp.float32)[..., None], axis=0)
    pod_low = pod_sum.reshape(owned_rows, -1).astype(jnp.bfloat16)
    all_rows = lax.all_gather(pod_low[None], "outer", axis=0, tiled=True)
    owned = jnp.sum(all_rows.astype(jnp.float32), axis=0)
    new_first = first_decay * first_moment + (1.0 - first_decay) * owned
    new_second = second_decay * second_moment + (1.0 - second_decay) * owned * owned
    corrected = new_first / (1.0 - first_decay**step_count)
    spread = jnp.sqrt(new_second / (1.0 - second_decay**step_count)) + 1e-08
    update = (corrected / spread).astype(jnp.bfloat16)
    gathered = lax.all_gather(update, "shard", axis=0, tiled=True)
    reordered = jnp.dot(projector, placing.T, preferred_element_type=jnp.float32).astype(
        jnp.bfloat16
    )
    change = jnp.dot(reordered, gathered, preferred_element_type=jnp.float32)
    new_weights = (weights.astype(jnp.float32) - update_scale * change).astype(jnp.bfloat16)
    return (new_weights, new_first, new_second)


def solution(mesh):
    placed = (
        P("outer", "shard", None, None),
        P("outer", "shard", None, None),
        P(),
        P(("outer", "shard"), None),
        P(("outer", "shard"), None),
        P("shard", None),
        P("shard", None),
    )
    return jax.shard_map(
        per_device,
        mesh=mesh,
        in_specs=placed,
        out_specs=(P(("outer", "shard"), None), P("shard", None), P("shard", None)),
        check_vma=False,
    )
```

profile of v0, /device:TPU:1, one launch (start us, length us, event | category | flops | bytes accessed | tf_op | source)
XLA Modules:
  0.0 366.5 jit_solution(17580511060379455319)
XLA Ops:
  7.2 0.0 copy-start
  7.2 0.7 iota_add_fusion
  7.9 0.2 convert_reduce_fusion.1
  8.1 0.0 copy-done
  8.1 0.2 convolution_convert_fusion.1
  8.3 0.7 copy.13
  9.0 10.0 %all-to-all-start.1 = ((bf16[32,8,116]{2,1,0:T(8,128)(2,1)}), bf16[32,8,116]{2,1,0:T(8,128)(2,1)S(1)}, u32[]{:S(2)}, u32[]{:S(2)}) async-start(bf16[32,8,116]{2,1,0:T(8,128)(2,1)} %bitcast.3), calls=%async_computation.1 | async-start | bytes 131072 | tf_op jit(solution)/shard_map/all_to_all | solution.py:36
  19.0 8.4 %fusion = bf16[32,8,14848]{2,1,0:T(8,128)(2,1)} fusion(bf16[1,1,256,14848]{3,2,1,0:T(8,128)(2,1)} %param.7, s32[256]{0:T(256)S(1)} %convert_reduce_fusion.1), kind=kOutput, calls=%fused_computation.1 | convolution fusion | flops 1950023680 | bytes 15205376 | tf_op jit(solution)/shard_map/dot_general | solution.py:26
  27.4 0.0 all-to-all-done.1
  27.4 7.8 %all-to-all-start = ((bf16[32,8,14848]{2,1,0:T(8,128)(2,1)}), bf16[32,8,14848]{2,1,0:T(8,128)(2,1)}, u32[]{:S(2)}, u32[]{:S(2)}) async-start(bf16[32,8,14848]{2,1,0:T(8,128)(2,1)} %fusion), calls=%async_computation | async-start | bytes 15204352 | tf_op jit(solution)/shard_map/all_to_all | solution.py:29
  35.2 0.0 copy-start.2
  35.2 0.0 all-gather.6.cloned.1.call-start
  35.3 0.4 copy.14
  35.7 0.0 copy-start.1
  35.7 0.0 copy-start.3
  35.7 166.9 %all-to-all-done = bf16[32,8,14848]{2,1,0:T(8,128)(2,1)} async-done(((bf16[32,8,14848]{2,1,0:T(8,128)(2,1)}), bf16[32,8,14848]{2,1,0:T(8,128)(2,1)}, u32[]{:S(2)}, u32[]{:S(2)}) %all-to-all-start) | async-done | bytes 7602208 | tf_op jit(solution)/shard_map/all_to_all | solution.py:29
  202.7 8.6 %fusion.3 = bf16[8,14848]{1,0:T(8,128)(2,1)} fusion(bf16[32,8,14848]{2,1,0:T(8,128)(2,1)} %all-to-all-done, f32[32,8,116]{1,2,0:T(8,128)S(1)} %copy.14), kind=kLoop, calls=%fused_computation.6 | loop fusion | flops 11284480 | bytes 7958528 | tf_op jit(solution)/shard_map/reduce_sum | solution.py:45
  211.2 0.0 all-gather.6.cloned.1.call-update
  211.3 0.0 all-gather.4.cloned.1.call-start
  211.3 71.3 %all-gather.6.cloned.1.call-done = bf16[64,14848]{1,0:T(8,128)(2,1)} async-done(((bf16[8,14848]{1,0:T(8,128)(2,1)}), bf16[64,14848]{1,0:T(8,128)(2,1)}) %all-gather.6.cloned.1.call-update) | async-done | bytes 1900560 | tf_op jit(solution)/shard_map/all_gather | solution.py:47
  282.6 1.8 convert_reduce_fusion
  284.4 0.0 copy-done.2
  284.4 2.2 divide_convert_fusion
  286.6 0.0 all-gather.4.cloned.1.call-update
  286.6 67.3 %all-gather.4.cloned.1.call-done = bf16[256,14848]{1,0:T(8,128)(2,1)} async-done(((bf16[8,14848]{1,0:T(8,128)(2,1)}), bf16[256,14848]{1,0:T(8,128)(2,1)}) %all-gather.4.cloned.1.call-update) | async-done | bytes 7602192 | tf_op jit(solution)/shard_map/all_gather | solution.py:54
  353.9 0.0 copy-done.1
  353.9 0.0 copy-done.3
  353.9 5.7 %fusion.2 = bf16[32,14848]{1,0:T(8,128)(2,1)} fusion(bf16[256,14848]{1,0:T(8,128)(2,1)} %all-gather.4.cloned.1.call-done, bf16[32,14848]{1,0:T(8,128)(2,1)S(1)} %copy-done.1, bf16[32,256]{1,0:T(8,128)(2,1)S(1)} %copy-done.3, s32[256]{0:T(256)S(1)} %convert_reduce_fusion.1), kind=kOutput, calls=%fused_computation.4 | convolution fusion | flops 249438208 | bytes 9520128 | tf_op jit(solution)/shard_map/dot_general | solution.py:58
Async XLA Ops:
  7.2 0.9 copy-start
  9.0 18.4 %all-to-all-start.1 = ((bf16[32,8,116]{2,1,0:T(8,128)(2,1)}), bf16[32,8,116]{2,1,0:T(8,128)(2,1)S(1)}, u32[]{:S(2)}, u32[]{:S(2)}) async-start(bf16[32,8,116]{2,1,0:T(8,128)(2,1)} %bitcast.3), calls=%async_computation.1 | async-start | bytes 131072 | tf_op jit(solution)/shard_map/all_to_all | solution.py:36
  27.4 175.2 %all-to-all-start = ((bf16[32,8,14848]{2,1,0:T(8,128)(2,1)}), bf16[32,8,14848]{2,1,0:T(8,128)(2,1)}, u32[]{:S(2)}, u32[]{:S(2)}) async-start(bf16[32,8,14848]{2,1,0:T(8,128)(2,1)} %fusion), calls=%async_computation | async-start | bytes 15204352 | tf_op jit(solution)/shard_map/all_to_all | solution.py:29
  35.2 249.2 %copy-start.2 = (f32[8,14848]{1,0:T(8,128)S(1)}, f32[8,14848]{1,0:T(8,128)}, u32[]{:S(2)}) copy-start(f32[8,14848]{1,0:T(8,128)} %param.12) | copy-start | bytes 1425412
  35.2 247.3 %all-gather.6.cloned.1.call-start = ((), (), s32[]{:S(2)}) async-start(), calls=%async_computation.3 | async-start | bytes 2138112 | tf_op jit(solution)/shard_map/all_gather | solution.py:47
  35.7 318.2 %copy-start.1 = (bf16[32,14848]{1,0:T(8,128)(2,1)S(1)}, bf16[32,14848]{1,0:T(8,128)(2,1)}, u32[]{:S(2)}) copy-start(bf16[32,14848]{1,0:T(8,128)(2,1)} %param.11) | copy-start | bytes 2850820
  35.7 318.2 %copy-start.3 = (bf16[32,256]{1,0:T(8,128)(2,1)S(1)}, bf16[32,256]{1,0:T(8,128)(2,1)}, u32[]{:S(2)}) copy-start(bf16[32,256]{1,0:T(8,128)(2,1)} %param.10) | copy-start | bytes 49156
  211.3 142.7 %all-gather.4.cloned.1.call-start = ((), (), s32[]{:S(2)}) async-start(), calls=%async_computation.2 | async-start | bytes 7839744 | tf_op jit(solution)/shard_map/all_gather | solution.py:54
Sparse Core Ops, SparseCore 0:
  211.4 71.1 all-gather.5
  286.8 67.1 all-gather.3
where the time goes:
time: 367 us
  waiting for transfers between devices  306 us (83%)
  starting transfers between devices  17.9 us (5%)
  matrix products  14.3 us (4%)
  between operations  14.1 us (4%)
  other arithmetic  13.5 us (4%)
    all_to_all x1, waiting for transfers between devices, per_device(): lax.all_to_all(sent_values.reshape(shards, owned_rows, -1), 'shard', spli...  167 us
    all_gather x1, waiting for transfers between devices, per_device(): all_rows = lax.all_gather(pod_low[None], 'outer', axis=0, tiled=True)  71.3 us
    all_gather x1, waiting for transfers between devices, per_device(): gathered = lax.all_gather(update, 'shard', axis=0, tiled=True)  67.3 us
    all_to_all x1, starting transfers between devices, per_device(): lax.all_to_all(sent_scales.reshape(shards, owned_rows, col_blocks), 'shar...  10 us
    reduce_sum x1, other arithmetic, per_device(): jnp.sum(blocked * got_scales.astype(jnp.float32)[..., None], axis=0)  8.58 us
    dot_general x1, matrix products, per_device(): jnp.dot(placing, values, preferred_element_type=jnp.float32)  8.39 us
    all_to_all x1, starting transfers between devices, per_device(): lax.all_to_all(sent_values.reshape(shards, owned_rows, -1), 'shard', spli...  7.78 us
  transfers between devices with their start and end apart: 4, of which 3 were waited for; matrix products, arithmetic and copies ran while one was open for 2% of the time, Pallas kernels for 0%

commit v1 on v0

--- a/solution.py
+++ b/solution.py
@@ -44,7 +44,9 @@
     blocked = got_values.reshape(shards, owned_rows, col_blocks, block_width).astype(jnp.float32)
     pod_sum = jnp.sum(blocked * got_scales.astype(jnp.float32)[..., None], axis=0)
     pod_low = pod_sum.reshape(owned_rows, -1).astype(jnp.bfloat16)
-    all_rows = lax.all_gather(pod_low[None], "outer", axis=0, tiled=True)
+    all_rows = jnp.concatenate(
+        lax.all_to_all(jnp.stack([pod_low[None]] * lax.axis_size("outer")), "outer", 0, 0), axis=0
+    )
     owned = jnp.sum(all_rows.astype(jnp.float32), axis=0)
     new_first = first_decay * first_moment + (1.0 - first_decay) * owned
     new_second = second_decay * second_moment + (1.0 - second_decay) * owned * owned

time: 367 us -> 346 us (0.943)
  waiting for transfers between devices: 306 us -> 234 us
  blocking collectives: 0 us -> 54.3 us
    all_gather x1 -> x0, waiting for transfers between devices: 71.3 us -> none  [per_device(): all_rows = lax.all_gather(pod_low[None], 'outer', axis=0, tiled=True)]
    all_to_all x0 -> x1, blocking collectives: none -> 54.3 us  [per_device(): lax.all_to_all(jnp.stack([pod_low[None]] * lax.axis_size('outer')), 'oute...]
  transfers between devices with their start and end apart: 4 -> 3, of which waited for: 3 -> 2; matrix products, arithmetic and copies ran while one was open for 2% -> 3% of each run, Pallas kernels for 0% -> 0%
where the time goes in v1:
time: 346 us
  waiting for transfers between devices  234 us (68%)
  blocking collectives  54.3 us (16%)
  starting transfers between devices  17.8 us (5%)
  matrix products  14.3 us (4%)
  between operations  14.1 us (4%)
  other arithmetic  10.2 us (3%)
    all_to_all x1, waiting for transfers between devices, per_device(): lax.all_to_all(sent_values.reshape(shards, owned_rows, -1), 'shard', spli...  167 us
    all_gather x1, waiting for transfers between devices, per_device(): gathered = lax.all_gather(update, 'shard', axis=0, tiled=True)  66.6 us
    all_to_all x1, blocking collectives, per_device(): lax.all_to_all(jnp.stack([pod_low[None]] * lax.axis_size('outer')), 'oute...  54.3 us
    all_to_all x1, starting transfers between devices, per_device(): lax.all_to_all(sent_scales.reshape(shards, owned_rows, col_blocks), 'shar...  10 us
    dot_general x1, matrix products, per_device(): jnp.dot(placing, values, preferred_element_type=jnp.float32)  8.37 us
    reduce_sum x1, other arithmetic, per_device(): jnp.sum(blocked * got_scales.astype(jnp.float32)[..., None], axis=0)  7.89 us
    all_to_all x1, starting transfers between devices, per_device(): lax.all_to_all(sent_values.reshape(shards, owned_rows, -1), 'shard', spli...  7.78 us
  transfers between devices with their start and end apart: 3, of which 2 were waited for; matrix products, arithmetic and copies ran while one was open for 3% of the time, Pallas kernels for 0%

profile of v1, /device:TPU:1, one launch (start us, length us, event | category | flops | bytes accessed | tf_op | source)
XLA Modules:
  0.0 345.7 jit_solution(13415896121396260854)
XLA Ops:
  7.2 0.0 copy-start
  7.2 0.7 iota_add_fusion
  7.9 0.2 convert_reduce_fusion.1
  8.1 0.0 copy-done
  8.1 0.2 convolution_convert_fusion.1
  8.3 0.7 copy.13
  9.0 10.0 %all-to-all-start.1 = ((bf16[32,8,116]{2,1,0:T(8,128)(2,1)}), bf16[32,8,116]{2,1,0:T(8,128)(2,1)S(1)}, u32[]{:S(2)}, u32[]{:S(2)}) async-start(bf16[32,8,116]{2,1,0:T(8,128)(2,1)} %bitcast.3), calls=%async_computation.1 | async-start | bytes 131072 | tf_op jit(solution)/shard_map/all_to_all | solution.py:36
  19.0 8.4 %fusion = bf16[32,8,14848]{2,1,0:T(8,128)(2,1)} fusion(bf16[1,1,256,14848]{3,2,1,0:T(8,128)(2,1)} %param.7, s32[256]{0:T(256)S(1)} %convert_reduce_fusion.1), kind=kOutput, calls=%fused_computation.1 | convolution fusion | flops 1950023680 | bytes 15205376 | tf_op jit(solution)/shard_map/dot_general | solution.py:26
  27.4 0.0 all-to-all-done.1
  27.4 7.8 %all-to-all-start = ((bf16[32,8,14848]{2,1,0:T(8,128)(2,1)}), bf16[32,8,14848]{2,1,0:T(8,128)(2,1)}, u32[]{:S(2)}, u32[]{:S(2)}) async-start(bf16[32,8,14848]{2,1,0:T(8,128)(2,1)} %fusion), calls=%async_computation | async-start | bytes 15204352 | tf_op jit(solution)/shard_map/all_to_all | solution.py:29
  35.2 0.0 all-gather.2.cloned.1.call-start
  35.2 0.4 copy.14
  35.7 0.0 copy-start.2
  35.7 0.0 copy-start.3
  35.7 167.0 %all-to-all-done = bf16[32,8,14848]{2,1,0:T(8,128)(2,1)} async-done(((bf16[32,8,14848]{2,1,0:T(8,128)(2,1)}), bf16[32,8,14848]{2,1,0:T(8,128)(2,1)}, u32[]{:S(2)}, u32[]{:S(2)}) %all-to-all-start) | async-done | bytes 7602208 | tf_op jit(solution)/shard_map/all_to_all | solution.py:29
  202.6 7.9 %fusion.3 = bf16[8,14848]{1,0:T(8,128)(2,1)S(1)} fusion(bf16[32,8,14848]{2,1,0:T(8,128)(2,1)} %all-to-all-done, f32[32,8,116]{1,2,0:T(8,128)S(1)} %copy.14), kind=kLoop, calls=%fused_computation.6 | loop fusion | flops 11284480 | bytes 7958528 | tf_op jit(solution)/shard_map/reduce_sum | solution.py:45
  210.5 0.0 copy-start.1
  210.5 0.0 copy-start.4
  210.5 0.1 stack.3
  210.7 54.3 %all_to_all.15 = bf16[8,1,8,14848]{3,2,1,0:T(8,128)(2,1)S(1)} all-to-all(bf16[8,1,8,14848]{3,2,1,0:T(8,128)(2,1)S(1)} %stack.3), channel_id=1, replica_groups=mesh['outer'=8,'shard'=32] {'outer'}, dimensions={0} | all-to-all | bytes 3801088 | tf_op jit(solution)/shard_map/all_to_all | solution.py:48
  265.0 0.3 convert_reduce_fusion
  265.2 0.0 copy-done.2
  265.2 0.0 copy-done.3
  265.3 1.2 divide_convert_fusion
  266.5 0.0 all-gather.2.cloned.1.call-update
  266.5 66.6 %all-gather.2.cloned.1.call-done = bf16[256,14848]{1,0:T(8,128)(2,1)} async-done(((bf16[8,14848]{1,0:T(8,128)(2,1)}), bf16[256,14848]{1,0:T(8,128)(2,1)}) %all-gather.2.cloned.1.call-update) | async-done | bytes 7602192 | tf_op jit(solution)/shard_map/all_gather | solution.py:56
  333.1 0.0 copy-done.1
  333.1 0.0 copy-done.4
  333.1 5.7 %fusion.2 = bf16[32,14848]{1,0:T(8,128)(2,1)} fusion(bf16[256,14848]{1,0:T(8,128)(2,1)} %all-gather.2.cloned.1.call-done, bf16[32,14848]{1,0:T(8,128)(2,1)S(1)} %copy-done.1, bf16[32,256]{1,0:T(8,128)(2,1)S(1)} %copy-done.4, s32[256]{0:T(256)S(1)} %convert_reduce_fusion.1), kind=kOutput, calls=%fused_computation.4 | convolution fusion | flops 249438208 | bytes 9520128 | tf_op jit(solution)/shard_map/dot_general | solution.py:60
Async XLA Ops:
  7.2 0.9 copy-start
  9.0 18.4 %all-to-all-start.1 = ((bf16[32,8,116]{2,1,0:T(8,128)(2,1)}), bf16[32,8,116]{2,1,0:T(8,128)(2,1)S(1)}, u32[]{:S(2)}, u32[]{:S(2)}) async-start(bf16[32,8,116]{2,1,0:T(8,128)(2,1)} %bitcast.3), calls=%async_computation.1 | async-start | bytes 131072 | tf_op jit(solution)/shard_map/all_to_all | solution.py:36
  27.4 175.2 %all-to-all-start = ((bf16[32,8,14848]{2,1,0:T(8,128)(2,1)}), bf16[32,8,14848]{2,1,0:T(8,128)(2,1)}, u32[]{:S(2)}, u32[]{:S(2)}) async-start(bf16[32,8,14848]{2,1,0:T(8,128)(2,1)} %fusion), calls=%async_computation | async-start | bytes 15204352 | tf_op jit(solution)/shard_map/all_to_all | solution.py:29
  35.2 297.9 %all-gather.2.cloned.1.call-start = ((), (), s32[]{:S(2)}) async-start(), calls=%async_computation.3 | async-start | bytes 7839744 | tf_op jit(solution)/shard_map/all_gather | solution.py:56
  35.7 229.6 %copy-start.2 = (f32[8,14848]{1,0:T(8,128)S(1)}, f32[8,14848]{1,0:T(8,128)}, u32[]{:S(2)}) copy-start(f32[8,14848]{1,0:T(8,128)} %param.12) | copy-start | bytes 1425412
  35.7 229.6 %copy-start.3 = (f32[8,14848]{1,0:T(8,128)S(1)}, f32[8,14848]{1,0:T(8,128)}, u32[]{:S(2)}) copy-start(f32[8,14848]{1,0:T(8,128)} %param.13) | copy-start | bytes 1425412
  210.5 122.6 %copy-start.1 = (bf16[32,14848]{1,0:T(8,128)(2,1)S(1)}, bf16[32,14848]{1,0:T(8,128)(2,1)}, u32[]{:S(2)}) copy-start(bf16[32,14848]{1,0:T(8,128)(2,1)} %param.11) | copy-start | bytes 2850820
  210.5 122.6 %copy-start.4 = (bf16[32,256]{1,0:T(8,128)(2,1)S(1)}, bf16[32,256]{1,0:T(8,128)(2,1)}, u32[]{:S(2)}) copy-start(bf16[32,256]{1,0:T(8,128)(2,1)} %param.10) | copy-start | bytes 49156
Sparse Core Ops, SparseCore 0:
  266.6 66.4 all-gather.1
